TPU v7x, 128 devices: a whole 4x4x4 slice. The times are simulated.
128 devices in a mesh: rep: 8 (over y_hi, x), tr: 8 (over y_lo, z), tc: 2 (over core).
Axes of the slice: x: 4, y: 4 (y_hi: 2, y_lo: 2; y = y_hi * 2 + y_lo), z: 4, core: 2. Of those that a mesh axis runs over, the one named last changes fastest.
Arguments:
- tokens: bfloat16 [512, 16, 8, 1600], P(('rep', 'tr'), None, None, 'tc'), may hold values from -6 to 6
- prefix_kv: bfloat16 [512, 256, 512], P(('rep', 'tr'), None, 'tc')
- ssm_state: float32 [512, 16, 3200], P(('rep', 'tr'), None, 'tc'), may hold values from -6 to 6
- conv_state: float32 [512, 3, 3200], P(('rep', 'tr'), None, 'tc'), may hold values from -6 to 6
- prefix_len: int32 [512], replicated, may hold values from 1 to 256
- group_size: int32 [512], replicated, may hold values from 8 to 16
- serve_replica: int32 [512], replicated, may hold values from 0 to 7, as said below
- in_gain: float32 [1600], P('tc'), may hold values from 0.5 to 1.5
- w_query: bfloat16 [1600, 1024], P(('rep', 'tr'), 'tc'), may hold values from -0.15625 to 0.15625
- w_keyval: bfloat16 [1600, 512], P(('rep', 'tr'), 'tc'), may hold values from -0.15625 to 0.15625
- w_inner: bfloat16 [1600, 2, 3200], P(('rep', 'tr'), None, 'tc'), may hold values from -0.15625 to 0.15625
- conv_weight: float32 [4, 3200], P(None, 'tc'), may hold values from -3 to 3
- conv_bias: float32 [3200], P('tc'), may hold values from -3 to 3
- w_xproj: bfloat16 [3200, 132], P('tc'), may hold values from -0.109375 to 0.109375
- dt_weight: bfloat16 [100, 3200], P(None, 'tc'), may hold values from -0.625 to 0.625
- dt_bias: float32 [3200], P('tc'), may hold values from -4.5 to -1
- decay_log: float32 [16, 3200], P(None, 'tc'), may hold values from -1 to 2.5
- skip_gain: float32 [3200], P('tc'), may hold values from 0.5 to 1.5
- w_attn_out: bfloat16 [1024, 1600], P('tc', ('rep', 'tr'))
- w_ssm_out: bfloat16 [3200, 1600], P('tc', ('rep', 'tr'))
- attn_gain: float32 [1600], replicated, may hold values from 0.5 to 1.5
- ssm_gain: float32 [1600], replicated, may hold values from 0.5 to 1.5
Outputs:
- mixed: bfloat16 [512, 16, 8, 1600], P(('rep', 'tr'), None, None, 'tc')
Inputs may be any that keep to these rules, and one draw needn't show every extreme that they name: `serve_replica`: within each aligned block of 8 groups every replica is named equally often.
All inputs are finite; a program needn't handle non-finite values.
Results may differ from a plain program's by a relative error of at most 0.013.
Values may be sent and summed in bfloat16 or wider, within the bound.
A program may use at most 192 MiB of HBM per device.

v0:
```python
import jax
import jax.numpy as jnp
from jax import lax
from jax.sharding import PartitionSpec as P

D = 1600
HD = 64
QH = 16
KVH = 4
EPSILON = 1e-06


def table_pick(served, table):
    matches = served[:, None] == jnp.arange(table.shape[0], dtype=jnp.int32)[None, :]
    return jnp.sum(jnp.where(matches, table[None, :], 0), axis=1)


def prefix_scores(group_query, key_block, length, score_scale):
    scores = (
        jnp.einsum("rtkjd,pkd->rtkjp", group_query, key_block, preferred_element_type=jnp.float32)
        * score_scale
    )
    positions = jnp.arange(key_block.shape[0], dtype=jnp.int32)
    return jnp.where(positions < length, scores, -jnp.inf)


def local(
    tokens,
    prefix_kv,
    ssm_state,
    conv_state,
    prefix_len,
    group_size,
    serve_replica,
    in_gain,
    w_query,
    w_keyval,
    w_inner,
    conv_weight,
    conv_bias,
    w_xproj,
    dt_weight,
    dt_bias,
    decay_log,
    skip_gain,
    w_attn_out,
    w_ssm_out,
    attn_gain,
    ssm_gain,
):
    rep_count = lax.axis_size("rep")
    my_replica = lax.axis_index("rep")
    row_axis = lax.axis_size("tr")
    my_row = lax.axis_index("tr")
    tensor_count = lax.axis_size("tc")
    tensor_index = lax.axis_index("tc")
    group_count, slot_count, new_count, width_part = tokens.shape
    pair_count = group_count // rep_count
    head_dim = HD
    kv_here = KVH // tensor_count
    per_kv = QH // KVH
    heads_here = QH // tensor_count
    score_scale = head_dim ** (-0.5)
    row_count = group_count * slot_count * new_count
    request_count = group_count * slot_count
    route_plan = serve_replica.reshape(rep_count, row_axis, group_count)
    column = lax.dynamic_index_in_dim(route_plan, my_row, 1, keepdims=False)
    orders = jnp.argsort(column, axis=1, stable=True)
    send_order = lax.dynamic_index_in_dim(orders, my_replica, 0, keepdims=False)
    picked = lax.dynamic_slice_in_dim(orders, my_replica * pair_count, pair_count, 1)
    block_ids = jnp.arange(rep_count, dtype=jnp.int32) * row_axis + my_row
    served = (block_ids[:, None] * group_count + picked).reshape(group_count)
    lengths = table_pick(served, prefix_len)
    live_sizes = table_pick(served, group_size)
    moved_tokens, moved_cache = (
        lax.all_to_all(
            jnp.take(tokens, send_order, axis=0), "rep", split_axis=0, concat_axis=0, tiled=True
        ),
        lax.all_to_all(
            jnp.take(prefix_kv, send_order, axis=0), "rep", split_axis=0, concat_axis=0, tiled=True
        ),
    )
    moved_state, moved_conv = (
        lax.all_to_all(
            jnp.take(ssm_state, send_order, axis=0).astype(jnp.bfloat16),
            "rep",
            split_axis=0,
            concat_axis=0,
            tiled=True,
        ).astype(jnp.float32),
        lax.all_to_all(
            jnp.take(conv_state, send_order, axis=0).astype(jnp.bfloat16),
            "rep",
            split_axis=0,
            concat_axis=0,
            tiled=True,
        ).astype(jnp.float32),
    )
    x_rows = moved_tokens.reshape(row_count, width_part).astype(jnp.float32)
    square_sums = lax.psum(jnp.sum(x_rows * x_rows, axis=1), "tc")
    inv_rms = lax.rsqrt(square_sums / D + EPSILON)
    normed_part = (x_rows * inv_rms[:, None] * in_gain[None, :]).astype(jnp.bfloat16)
    normed = lax.all_gather(normed_part, "tc", axis=1, tiled=True)
    channels = w_inner.shape[2]
    inner_cols = w_inner.reshape(w_inner.shape[0], 2 * channels)
    pieces = (
        lax.all_gather(w_query, ("rep", "tr"), axis=0, tiled=True),
        lax.all_gather(w_keyval, ("rep", "tr"), axis=0, tiled=True),
        lax.all_gather(inner_cols, ("rep", "tr"), axis=0, tiled=True),
    )
    query_run = jnp.dot(normed, pieces[0], preferred_element_type=jnp.float32)
    keyval_run = jnp.dot(normed, pieces[1], preferred_element_type=jnp.float32)
    inner_run = jnp.dot(normed, pieces[2], preferred_element_type=jnp.float32)
    query = query_run.astype(jnp.bfloat16).reshape(
        group_count, slot_count, new_count, kv_here, per_kv, head_dim
    )
    keyval = keyval_run.astype(jnp.bfloat16).reshape(
        group_count, slot_count, new_count, kv_here, 2, head_dim
    )
    cache_len = moved_cache.shape[1]
    cache_heads = moved_cache.reshape(group_count, cache_len, kv_here, 2, head_dim)
    causal = jnp.arange(new_count)[None, :] <= jnp.arange(new_count)[:, None]

    def attend(group_args):
        group_query, group_kv, group_cache, length = group_args
        key_all = group_cache[:, :, 0]
        value_all = group_cache[:, :, 1]
        own_scores = (
            jnp.einsum(
                "rtkjd,rskd->rtkjs",
                group_query,
                group_kv[:, :, :, 0],
                preferred_element_type=jnp.float32,
            )
            * score_scale
        )
        own_scores = jnp.where(causal[None, :, None, None, :], own_scores, -jnp.inf)
        own_max = jnp.max(own_scores, axis=4)
        scores = prefix_scores(group_query, key_all, length, score_scale)
        row_max = jnp.maximum(jnp.max(scores, axis=4), own_max)
        prefix_weights = jnp.exp(scores - row_max[..., None])
        row_totals = jnp.sum(prefix_weights, axis=4)
        weighted = jnp.einsum(
            "rtkjp,pkd->rtkjd",
            prefix_weights.astype(jnp.bfloat16),
            value_all,
            preferred_element_type=jnp.float32,
        )
        own_weights = jnp.exp(own_scores - row_max[..., None])
        row_totals = row_totals + jnp.sum(own_weights, axis=4)
        weighted = weighted + jnp.einsum(
            "rtkjs,rskd->rtkjd",
            own_weights.astype(jnp.bfloat16),
            group_kv[:, :, :, 1],
            preferred_element_type=jnp.float32,
        )
        return (
            (weighted / row_totals[..., None])
            .astype(jnp.bfloat16)
            .reshape(slot_count, new_count, heads_here * head_dim)
        )

    heads = lax.map(attend, (query, keyval, cache_heads, lengths)).reshape(
        row_count, heads_here * head_dim
    )
    inner = inner_run.reshape(group_count, slot_count, new_count, 2, channels)
    conv_in = inner[:, :, :, 0]
    gate = inner[:, :, :, 1].reshape(row_count, channels)
    history = jnp.broadcast_to(
        moved_conv[:, None], (group_count, slot_count, moved_conv.shape[1], channels)
    )
    sequence = jnp.concatenate([history, conv_in], axis=2)
    conv_sum = jnp.broadcast_to(conv_bias, (group_count, slot_count, new_count, channels))
    for tap_index in range(conv_weight.shape[0]):
        conv_sum = (
            conv_sum + conv_weight[tap_index] * sequence[:, :, tap_index : tap_index + new_count]
        )
    conv_out = jax.nn.silu(conv_sum).astype(jnp.bfloat16).reshape(row_count, channels)
    projected = lax.psum(
        jnp.dot(conv_out, w_xproj, preferred_element_type=jnp.float32).astype(jnp.bfloat16), "tc"
    ).astype(jnp.float32)
    rank_width = dt_weight.shape[0]
    state_size = decay_log.shape[0]
    step_in = projected[:, :rank_width].astype(jnp.bfloat16)
    input_mix = projected[:, rank_width : rank_width + state_size]
    output_mix = projected[:, rank_width + state_size :]
    step_size = jax.nn.softplus(
        jnp.dot(step_in, dt_weight, preferred_element_type=jnp.float32) + dt_bias
    )
    decay_rate = -jnp.exp(decay_log)

    def token_major(values):
        return values.reshape(request_count, new_count, values.shape[1]).swapaxes(0, 1)

    start_state = jnp.broadcast_to(
        moved_state[:, None], (group_count, slot_count, state_size, channels)
    ).reshape(request_count, state_size, channels)

    def advance(carried, inputs):
        step_now, value_now, mix_in, mix_out = inputs
        carried = (
            jnp.exp(step_now[:, None, :] * decay_rate[None]) * carried
            + (step_now * value_now)[:, None, :] * mix_in[:, :, None]
        )
        result = jnp.sum(carried * mix_out[:, :, None], axis=1) + skip_gain * value_now
        return (carried, result)

    last_state, outputs = lax.scan(
        advance,
        start_state,
        (
            token_major(step_size),
            token_major(conv_out.astype(jnp.float32)),
            token_major(input_mix),
            token_major(output_mix),
        ),
    )
    ssm_out = outputs.swapaxes(0, 1).reshape(row_count, channels)
    gated = (ssm_out * jax.nn.silu(gate)).astype(jnp.bfloat16)
    pieces = (
        lax.all_gather(w_attn_out, ("rep", "tr"), axis=1, tiled=True),
        lax.all_gather(w_ssm_out, ("rep", "tr"), axis=1, tiled=True),
    )
    attn_part = jnp.dot(heads, pieces[0], preferred_element_type=jnp.float32)
    ssm_part = jnp.dot(gated, pieces[1], preferred_element_type=jnp.float32)
    attn_cols, ssm_cols = (
        lax.psum_scatter(
            attn_part.astype(jnp.bfloat16), "tc", scatter_dimension=1, tiled=True
        ).astype(jnp.float32),
        lax.psum_scatter(
            ssm_part.astype(jnp.bfloat16), "tc", scatter_dimension=1, tiled=True
        ).astype(jnp.float32),
    )
    attn_sq, ssm_sq = lax.psum(
        (jnp.sum(attn_cols * attn_cols, axis=1), jnp.sum(ssm_cols * ssm_cols, axis=1)), "tc"
    )
    attn_share = lax.dynamic_slice_in_dim(attn_gain, tensor_index * width_part, width_part, 0)
    ssm_share = lax.dynamic_slice_in_dim(ssm_gain, tensor_index * width_part, width_part, 0)
    attn_rms = lax.rsqrt(attn_sq / D + EPSILON)[:, None]
    ssm_rms = lax.rsqrt(ssm_sq / D + EPSILON)[:, None]
    branch = 0.5 * (attn_share * attn_cols * attn_rms + ssm_share * ssm_cols * ssm_rms)
    live = jnp.arange(slot_count)[None, :] < live_sizes[:, None]
    live_rows = jnp.broadcast_to(live[:, :, None], (group_count, slot_count, new_count)).reshape(
        row_count, 1
    )
    mixed = jnp.where(live_rows, x_rows + branch, 0.0).astype(jnp.bfloat16)
    return mixed.reshape(group_count, slot_count, new_count, width_part)


def solution(mesh):
    placed = (
        P(("rep", "tr"), None, None, "tc"),
        P(("rep", "tr"), None, "tc"),
        P(("rep", "tr"), None, "tc"),
        P(("rep", "tr"), None, "tc"),
        P(),
        P(),
        P(),
        P("tc"),
        P(("rep", "tr"), "tc"),
        P(("rep", "tr"), "tc"),
        P(("rep", "tr"), None, "tc"),
        P(None, "tc"),
        P("tc"),
        P("tc", None),
        P(None, "tc"),
        P("tc"),
        P(None, "tc"),
        P("tc"),
        P("tc", ("rep", "tr")),
        P("tc", ("rep", "tr")),
        P(),
        P(),
    )
    return jax.shard_map(
        local,
        mesh=mesh,
        in_specs=placed,
        out_specs=P(("rep", "tr"), None, None, "tc"),
        check_vma=False,
    )
```

profile of v0, /device:TPU:1, one launch (start us, length us, event | category | flops | bytes accessed | tf_op | source)
XLA Modules:
  0.0 1650.3 jit_solution(8832406001314647902)
XLA Ops:
  13.5 32.2 %all_to_all.20 = bf16[8,16,8,800]{3,2,1,0:T(8,128)(2,1)S(1)} all-to-all(bf16[8,16,8,800]{3,2,1,0:T(8,128)(2,1)S(1)} %broadcast_select_fusion), channel_id=1, replica_groups=mesh['rep'=8,'tr'=8,'tc'=2] {'rep'}, dimensions={0} | all-to-all | bytes 3276800 | tf_op jit(solution)/shard_map/all_to_all | solution.py:76
  64.8 163.2 %all-gather.1 = bf16[64,25,256]{2,1,0:T(8,128)(2,1)S(1)} all-gather(bf16[1,25,256]{2,1,0:T(8,128)(2,1)S(1)} %bitcast.200), channel_id=1, replica_groups=mesh['rep'=8,'tr'=8,'tc'=2] {'rep','tr'}, dimensions={0}, use_global_device_ids=true | all-gather | bytes 832000 | tf_op jit(solution)/shard_map/all_gather | solution.py:108
  239.3 64.2 %all-gather.13.cloned.1.call-done = bf16[64,25,512]{2,1,0:T(8,128)(2,1)} async-done(((bf16[1,25,512]{2,1,0:T(8,128)(2,1)}), bf16[64,25,512]{2,1,0:T(8,128)(2,1)}) %all-gather.13.cloned.1.call-update) | async-done | bytes 1638416 | tf_op jit(solution)/shard_map/all_gather | solution.py:107
  306.1 327.9 %all-gather.15.cloned.1.call-done = bf16[64,25,512]{2,1,0:T(8,128)(2,1)} async-done(((bf16[1,25,512]{2,1,0:T(8,128)(2,1)}), bf16[64,25,512]{2,1,0:T(8,128)(2,1)}) %all-gather.15.cloned.1.call-update) | async-done | bytes 1638416 | tf_op jit(solution)/shard_map/all_gather | solution.py:221
  637.6 58.4 %all-gather.11.cloned.1.call-done = bf16[1024,1600]{0,1:T(8,128)(2,1)} async-done(((bf16[1024,800]{0,1:T(8,128)(2,1)}), bf16[1024,1600]{0,1:T(8,128)(2,1)}) %all-gather.11.cloned.1.call-update) | async-done | bytes 3276816 | tf_op jit(solution)/shard_map/all_gather | solution.py:103
  706.8 69.8 %while.24 = (s32[]{:T(128)}, bf16[8,16,8,512]{3,2,1,0:T(8,128)(2,1)}, bf16[8,256,2,2,64]{1,4,3,2,0:T(8,128)(2,1)}, s32[8]{0:T(128)S(1)}, bf16[8,16,8,2,4,64]{5,4...) while((s32[]{:T(128)}, bf16[8,16,8,512]{3,2,1,0:T(8,128)(2,1)}, ...), condition=%wide.region_10.11_spmd.clone, body=%wide.region_5.10_spmd.clone.sunk | while | flops 71293248 | bytes 7227317 | solution.py:163
  776.6 234.6 %all-gather.17.cloned.1.call-done = bf16[64,25,3200]{2,1,0:T(8,128)(2,1)} async-done(((bf16[1,25,3200]{2,1,0:T(8,128)(2,1)}), bf16[64,25,3200]{2,1,0:T(8,128)(2,1)}) %all-gather.17.cloned.1.call-update) | async-done | bytes 10240016 | tf_op jit(solution)/shard_map/all_gather | solution.py:109
  1011.2 11.8 reshape.228
  1023.0 19.0 %fusion.52 = f32[1024,3200]{1,0:T(8,128)} fusion(bf16[1024,1600]{0,1:T(8,128)(2,1)} %all-gather.11.cloned.1.call-done, bf16[1600,3200]{1,0:T(8,128)(2,1)} %reshape.228), kind=kOutput, calls=%fused_computation.124 | convolution fusion | flops 10485760000 | bytes 26624000 | tf_op jit(solution)/shard_map/dot_general | solution.py:113
  1042.0 17.6 %reshape.180 = f32[8,16,8,2,1600]{4,3,2,1,0:T(2,128)} reshape(f32[1024,3200]{1,0:T(8,128)} %fusion.52) | data formatting | bytes 26214400 | tf_op jit(solution)/shard_map/reshape | solution.py:166
  1059.6 16.1 fusion.50
  1082.8 15.4 multiply_convert_fusion
  1106.9 247.1 %all-gather.19.cloned.1.call-done = bf16[64,25,1600]{2,1,0:T(8,128)(2,1)} async-done(((bf16[1,25,1600]{2,1,0:T(8,128)(2,1)}), bf16[64,25,1600]{2,1,0:T(8,128)(2,1)}) %all-gather.19.cloned.1.call-update) | async-done | bytes 5120016 | tf_op jit(solution)/shard_map/all_gather | solution.py:222
  1354.0 8.8 reshape.230
  1362.8 5.3 copy.170
  1368.2 6.3 copy.192
  1374.4 46.0 %all-reduce.3.cloned.1.call-done = bf16[1024,132]{0,1:T(8,128)(2,1)} async-done(((bf16[1024,132]{0,1:T(8,128)(2,1)}), bf16[1024,132]{0,1:T(8,128)(2,1)}) %all-reduce.3.cloned.1.call-update) | async-done | bytes 270352 | tf_op jit(solution)/shard_map/psum | solution.py:179
  1420.5 7.6 compare_select_fusion
  1428.0 7.5 copy.169
  1436.8 5.9 broadcast_in_dim.164
  1442.7 155.4 %while.23 = (s32[]{:T(128)}, f32[128,16,1600]{2,1,0:T(8,128)}, f32[8,128,1600]{2,1,0:T(8,128)}, f32[8,128,1600]{2,0,1:T(8,128)}, f32[16,1600]{1,0:T(8,128)S(1)},...) while((s32[]{:T(128)}, f32[128,16,1600]{2,1,0:T(8,128)}, ...), condition=%wide.region_17.18_spmd, body=%wide.region_15.17_spmd.sunk | while | flops 20070400 | bytes 37087612 | solution.py:208
  1447.7 12.3 multiply_reduce_fusion.3
  1467.1 12.3 multiply_reduce_fusion.3
  1486.4 12.3 multiply_reduce_fusion.3
  1505.9 12.3 multiply_reduce_fusion.3
  1525.3 12.3 multiply_reduce_fusion.3
  1544.7 12.3 multiply_reduce_fusion.3
  1564.2 12.3 multiply_reduce_fusion.3
  1583.7 12.3 multiply_reduce_fusion.3
  1598.1 8.8 fusion.34
  1607.0 10.2 convolution_convert_fusion
  1624.6 7.8 reduce-scatter.5.cloned.1.call-done
  (339 shorter events, 215.4 us)
Async XLA Ops:
  6.5 3.3 copy-start
  6.5 297.0 %all-gather.13.cloned.1.call-start = ((), (), s32[]{:S(2)}) async-start(), calls=%async_computation.10 | async-start | bytes 2129920 | tf_op jit(solution)/shard_map/all_gather | solution.py:107
  7.3 626.7 %all-gather.15.cloned.1.call-start = ((), (), s32[]{:S(2)}) async-start(), calls=%async_computation.11 | async-start | bytes 2129920 | tf_op jit(solution)/shard_map/all_gather | solution.py:221
  8.0 42.6 %copy-start.12 = (f32[800]{0:T(1024)S(1)}, f32[800]{0:T(1024)}, u32[]{:S(2)}) copy-start(f32[800]{0:T(1024)} %param.33) | copy-start | bytes 9604
  8.0 688.0 %all-gather.11.cloned.1.call-start = ((), (), s32[]{:S(2)}) async-start(), calls=%async_computation.6 | async-start | bytes 4915200 | tf_op jit(solution)/shard_map/all_gather | solution.py:103
  46.2 11.2 copy-start.7
  46.2 12.2 copy-start.5
  53.6 11.3 copy-start.10
  57.3 173.7 %copy-start.3 = (f32[8,3,1600]{2,0,1:T(8,128)S(1)}, f32[8,3,1600]{2,0,1:T(8,128)}, u32[]{:S(2)}) copy-start(f32[8,3,1600]{2,0,1:T(8,128)} %param.29) | copy-start | bytes 460804
  57.3 175.2 %copy-start.9 = (f32[4,1600]{1,0:T(4,128)S(1)}, f32[4,1600]{1,0:T(4,128)}, u32[]{:S(2)}) copy-start(f32[4,1600]{1,0:T(4,128)} %param.37) | copy-start | bytes 76804
  57.3 175.3 %copy-start.15 = (s32[512]{0:T(512)S(1)}, s32[512]{0:T(512)}, u32[]{:S(2)}) copy-start(s32[512]{0:T(512)} %param.31) | copy-start | bytes 6148
  57.3 175.3 %copy-start.16 = (s32[512]{0:T(512)S(1)}, s32[512]{0:T(512)}, u32[]{:S(2)}) copy-start(s32[512]{0:T(512)} %param.30) | copy-start | bytes 6148
  57.3 176.0 %copy-start.8 = (f32[16,1600]{1,0:T(8,128)S(1)}, f32[16,1600]{1,0:T(8,128)}, u32[]{:S(2)}) copy-start(f32[16,1600]{1,0:T(8,128)} %param.42) | copy-start | bytes 307204
  57.4 953.8 %all-gather.17.cloned.1.call-start = ((), (), s32[]{:S(2)}) async-start(), calls=%async_computation.12 | async-start | bytes 13312000 | tf_op jit(solution)/shard_map/all_gather | solution.py:109
  60.2 174.1 %all-to-all-start.1 = ((bf16[8,256,256]{2,1,0:T(8,128)(2,1)}), bf16[8,256,256]{2,1,0:T(8,128)(2,1)S(1)}, u32[]{:S(2)}, u32[]{:S(2)}) async-start(bf16[8,256,256]{2,1,0:T(8,128)(2,1)} %broadcast_select_fusion.1), calls=%async_computation.1 | async-start | bytes 2097152 | tf_op jit(solution)/shard_map/all_to_all | solution.py:79
  64.2 1289.9 %all-gather.19.cloned.1.call-start = ((), (), s32[]{:S(2)}) async-start(), calls=%async_computation.13 | async-start | bytes 6922240 | tf_op jit(solution)/shard_map/all_gather | solution.py:222
  234.3 844.7 %all-to-all-start.3 = ((bf16[8,3,1600]{2,1,0:T(4,128)(2,1)}), bf16[8,3,1600]{2,1,0:T(4,128)(2,1)S(1)}, u32[]{:S(2)}, u32[]{:S(2)}) async-start(bf16[8,3,1600]{2,1,0:T(4,128)(2,1)} %copy.168), calls=%async_computation.4 | async-start | bytes 212992 | tf_op jit(solution)/shard_map/all_to_all | solution.py:91
  1075.7 7.1 copy-start.11
  1079.0 357.8 %all-to-all-start.2 = ((bf16[8,16,1600]{2,1,0:T(8,128)(2,1)}), bf16[8,16,1600]{2,1,0:T(8,128)(2,1)S(1)}, u32[]{:S(2)}, u32[]{:S(2)}) async-start(bf16[8,16,1600]{2,1,0:T(8,128)(2,1)} %select_convert_fusion), calls=%async_computation.3 | async-start | bytes 851968 | tf_op jit(solution)/shard_map/all_to_all | solution.py:84
  1082.5 338.0 %all-reduce.3.cloned.1.call-start = ((), (), s32[]{:S(2)}) async-start(), calls=%async_computation.8 | async-start | bytes 557056 | tf_op jit(solution)/shard_map/psum | solution.py:179
  1082.8 17.1 %copy-start.18 = (bf16[1600,132]{0,1:T(8,128)(2,1)S(1)}, bf16[1600,132]{0,1:T(8,128)(2,1)}, u32[]{:S(2)}) copy-start(bf16[1600,132]{0,1:T(8,128)(2,1)} %param.39) | copy-start | bytes 1267204
  1082.8 19.2 %copy-start.4 = (bf16[1600,512]{1,0:T(8,128)(2,1)S(1)}, bf16[1600,512]{1,0:T(8,128)(2,1)}, u32[]{:S(2)}) copy-start(bf16[1600,512]{1,0:T(8,128)(2,1)} %reshape.226) | copy-start | bytes 4915204
  1098.2 1.7 copy-start.2
  1102.0 520.7 %reduce-scatter.3.cloned.1.call-start = ((), (), s32[]{:S(2)}) async-start(), calls=%async_computation.7 | async-start | bytes 4915200 | tf_op jit(solution)/shard_map/reduce_scatter | solution.py:227
  1106.9 525.5 %reduce-scatter.5.cloned.1.call-start = ((), (), s32[]{:S(2)}) async-start(), calls=%async_computation.9 | async-start | bytes 4915200 | tf_op jit(solution)/shard_map/reduce_scatter | solution.py:230
  1368.1 52.3 %copy-start.19 = (bf16[100,1600]{1,0:T(8,128)(2,1)S(1)}, bf16[100,1600]{1,0:T(8,128)(2,1)}, u32[]{:S(2)}) copy-start(bf16[100,1600]{1,0:T(8,128)(2,1)} %param.40) | copy-start | bytes 960004
  1368.2 52.3 %copy-start.20 = (f32[1600]{0:T(1024)S(1)}, f32[1600]{0:T(1024)}, u32[]{:S(2)}) copy-start(f32[1600]{0:T(1024)} %param.41) | copy-start | bytes 19204
  1436.8 5.9 copy-start.6
  1607.0 10.3 copy-start.13
  1607.0 10.4 copy-start.14
  1607.0 10.4 copy-start.17
  1622.6 20.6 %copy-start.1 = (bf16[8,16,8,800]{3,2,1,0:T(8,128)(2,1)S(1)}, bf16[8,16,8,800]{3,2,1,0:T(8,128)(2,1)}, u32[]{:S(2)}) copy-start(bf16[8,16,8,800]{3,2,1,0:T(8,128)(2,1)} %param.26) | copy-start | bytes 4915204
Sparse Core Ops, SparseCore 0:
  9.0 294.4 all-gather.12
  305.2 328.7 all-gather.14
  635.6 60.3 all-gather.10
  697.5 313.6 all-gather.16
  1012.7 341.3 all-gather.18
  1356.3 64.0 all-reduce.2
  1422.9 14.9 reduce-scatter.2
  1617.4 14.9 reduce-scatter.4
where the time goes:
time: 1660 us; the launch traced here: 1650 us
  waiting for transfers between devices  988 us (60%)
  blocking collectives  202 us (12%)
  local copies, waits for them, and re-layouts  186 us (11%)
  other arithmetic  177 us (11%)
  matrix products  71.2 us (4%)
    all_gather x1, waiting for transfers between devices, local(): lax.all_gather(w_attn_out, ('rep', 'tr'), axis=1, tiled=True)  328 us
    all_gather x1, waiting for transfers between devices, local(): lax.all_gather(w_ssm_out, ('rep', 'tr'), axis=1, tiled=True)  247 us
    all_gather x1, waiting for transfers between devices, local(): lax.all_gather(inner_cols, ('rep', 'tr'), axis=0, tiled=True)  235 us
    all_gather x1, blocking collectives, local(): lax.all_gather(w_keyval, ('rep', 'tr'), axis=0, tiled=True)  163 us
    reduce_sum x8, other arithmetic, advance(): jnp.sum(carried * mix_out[:, :, None], axis=1) + skip_gain * value_now  98.4 us
    all_gather x1, waiting for transfers between devices, local(): lax.all_gather(w_query, ('rep', 'tr'), axis=0, tiled=True)  64.2 us
    all_gather x1, waiting for transfers between devices, local(): normed = lax.all_gather(normed_part, 'tc', axis=1, tiled=True)  58.4 us
    psum x1, waiting for transfers between devices, local(): lax.psum(jnp.dot(conv_out, w_xproj, preferred_element_type=jnp.float32).a...  46 us
  transfers between devices with their start and end apart: 11, of which 7 were waited for; matrix products, arithmetic and copies ran while one was open for 26% of the time, Pallas kernels for 0%

commit v1 on v0

--- a/solution.py
+++ b/solution.py
@@ -176,8 +176,12 @@
             conv_sum + conv_weight[tap_index] * sequence[:, :, tap_index : tap_index + new_count]
         )
     conv_out = jax.nn.silu(conv_sum).astype(jnp.bfloat16).reshape(row_count, channels)
-    projected = lax.psum(
-        jnp.dot(conv_out, w_xproj, preferred_element_type=jnp.float32).astype(jnp.bfloat16), "tc"
+    projected = jnp.sum(
+        lax.all_gather(
+            jnp.dot(conv_out, w_xproj, preferred_element_type=jnp.float32).astype(jnp.bfloat16),
+            "tc",
+        ),
+        axis=0,
     ).astype(jnp.float32)
     rank_width = dt_weight.shape[0]
     state_size = decay_log.shape[0]

time: 1660 us -> 1730 us (1.042)
  blocking collectives: 202 us -> 246 us
  waiting for transfers between devices: 988 us -> 1020 us
    all_gather x1, waiting for transfers between devices: 235 us -> 347 us  [local(): lax.all_gather(inner_cols, ('rep', 'tr'), axis=0, tiled=True)]
    psum x1 -> x0, waiting for transfers between devices: 46 us -> none  [local(): lax.psum(jnp.dot(conv_out, w_xproj, preferred_element_type=jnp.float32).a...]
    all_gather x0 -> x1, blocking collectives: none -> 44.3 us  [local(): lax.all_gather(jnp.dot(conv_out, w_xproj, preferred_element_type=jnp.floa...]
    all_gather x1, waiting for transfers between devices: 247 us -> 215 us  [local(): lax.all_gather(w_ssm_out, ('rep', 'tr'), axis=1, tiled=True)]
    unnamed x50 -> x56, local copies, waits for them, and re-layouts: 40.4 us -> 38.9 us
  transfers between devices with their start and end apart: 11 -> 10, of which waited for: 7 -> 6; matrix products, arithmetic and copies ran while one was open for 26% -> 24% of each run, Pallas kernels for 0% -> 0%
where the time goes in v1:
time: 1730 us; the launch traced here: 1720 us
  waiting for transfers between devices  1020 us (59%)
  blocking collectives  246 us (14%)
  local copies, waits for them, and re-layouts  182 us (11%)
  other arithmetic  178 us (10%)
  matrix products  67.9 us (4%)
    all_gather x1, waiting for transfers between devices, local(): lax.all_gather(inner_cols, ('rep', 'tr'), axis=0, tiled=True)  347 us
    all_gather x1, waiting for transfers between devices, local(): lax.all_gather(w_attn_out, ('rep', 'tr'), axis=1, tiled=True)  326 us
    all_gather x1, waiting for transfers between devices, local(): lax.all_gather(w_ssm_out, ('rep', 'tr'), axis=1, tiled=True)  215 us
    all_gather x1, blocking collectives, local(): lax.all_gather(w_keyval, ('rep', 'tr'), axis=0, tiled=True)  163 us
    reduce_sum x8, other arithmetic, advance(): jnp.sum(carried * mix_out[:, :, None], axis=1) + skip_gain * value_now  98.8 us
    all_gather x1, waiting for transfers between devices, local(): lax.all_gather(w_query, ('rep', 'tr'), axis=0, tiled=True)  65.8 us
    all_gather x1, waiting for transfers between devices, local(): normed = lax.all_gather(normed_part, 'tc', axis=1, tiled=True)  58.4 us
    all_gather x1, blocking collectives, local(): lax.all_gather(jnp.dot(conv_out, w_xproj, preferred_element_type=jnp.floa...  44.3 us
  transfers between devices with their start and end apart: 10, of which 6 were waited for; matrix products, arithmetic and copies ran while one was open for 24% of the time, Pallas kernels for 0%

profile of v1, /device:TPU:1, one launch (start us, length us, event | category | flops | bytes accessed | tf_op | source)
XLA Modules:
  0.0 1724.4 jit_solution(13276612273961805889)
XLA Ops:
  13.5 32.2 %all_to_all.20 = bf16[8,16,8,800]{3,2,1,0:T(8,128)(2,1)S(1)} all-to-all(bf16[8,16,8,800]{3,2,1,0:T(8,128)(2,1)S(1)} %broadcast_select_fusion), channel_id=1, replica_groups=mesh['rep'=8,'tr'=8,'tc'=2] {'rep'}, dimensions={0} | all-to-all | bytes 3276800 | tf_op jit(solution)/shard_map/all_to_all | solution.py:76
  64.8 162.6 %all-gather.2 = bf16[64,25,256]{2,1,0:T(8,128)(2,1)S(1)} all-gather(bf16[1,25,256]{2,1,0:T(8,128)(2,1)S(1)} %bitcast.204), channel_id=1, replica_groups=mesh['rep'=8,'tr'=8,'tc'=2] {'rep','tr'}, dimensions={0}, use_global_device_ids=true | all-gather | bytes 832000 | tf_op jit(solution)/shard_map/all_gather | solution.py:108
  238.9 65.8 %all-gather.14.cloned.1.call-done = bf16[64,25,512]{2,1,0:T(8,128)(2,1)} async-done(((bf16[1,25,512]{2,1,0:T(8,128)(2,1)}), bf16[64,25,512]{2,1,0:T(8,128)(2,1)}) %all-gather.14.cloned.1.call-update) | async-done | bytes 1638416 | tf_op jit(solution)/shard_map/all_gather | solution.py:107
  307.3 326.2 %all-gather.16.cloned.1.call-done = bf16[64,25,512]{2,1,0:T(8,128)(2,1)} async-done(((bf16[1,25,512]{2,1,0:T(8,128)(2,1)}), bf16[64,25,512]{2,1,0:T(8,128)(2,1)}) %all-gather.16.cloned.1.call-update) | async-done | bytes 1638416 | tf_op jit(solution)/shard_map/all_gather | solution.py:225
  637.2 58.4 %all-gather.12.cloned.1.call-done = bf16[1024,1600]{0,1:T(8,128)(2,1)} async-done(((bf16[1024,800]{0,1:T(8,128)(2,1)}), bf16[1024,1600]{0,1:T(8,128)(2,1)}) %all-gather.12.cloned.1.call-update) | async-done | bytes 3276816 | tf_op jit(solution)/shard_map/all_gather | solution.py:103
  706.4 69.8 %while.24 = (s32[]{:T(128)}, bf16[8,16,8,512]{3,2,1,0:T(8,128)(2,1)}, bf16[8,256,2,2,64]{1,4,3,2,0:T(8,128)(2,1)}, s32[8]{0:T(128)S(1)}, bf16[8,16,8,2,4,64]{5,4...) while((s32[]{:T(128)}, bf16[8,16,8,512]{3,2,1,0:T(8,128)(2,1)}, ...), condition=%wide.region_10.11_spmd.clone, body=%wide.region_5.10_spmd.clone.sunk | while | flops 71293248 | bytes 7227317 | solution.py:163
  776.2 5.5 convolution_convert_fusion.1
  781.7 215.2 %all-gather.20.cloned.1.call-done = bf16[64,25,1600]{2,1,0:T(8,128)(2,1)} async-done(((bf16[1,25,1600]{2,1,0:T(8,128)(2,1)}), bf16[64,25,1600]{2,1,0:T(8,128)(2,1)}) %all-gather.20.cloned.1.call-update) | async-done | bytes 5120016 | tf_op jit(solution)/shard_map/all_gather | solution.py:226
  996.9 8.6 reshape.231
  1005.5 346.9 %all-gather.18.cloned.1.call-done = bf16[64,25,3200]{2,1,0:T(8,128)(2,1)} async-done(((bf16[1,25,3200]{2,1,0:T(8,128)(2,1)}), bf16[64,25,3200]{2,1,0:T(8,128)(2,1)}) %all-gather.18.cloned.1.call-update) | async-done | bytes 10240016 | tf_op jit(solution)/shard_map/all_gather | solution.py:109
  1352.4 11.9 reshape.229
  1364.3 19.3 %fusion.52 = f32[1024,3200]{1,0:T(8,128)} fusion(bf16[1024,1600]{0,1:T(8,128)(2,1)} %all-gather.12.cloned.1.call-done, bf16[1600,3200]{1,0:T(8,128)(2,1)} %reshape.229), kind=kOutput, calls=%fused_computation.124 | convolution fusion | flops 10485760000 | bytes 26624000 | tf_op jit(solution)/shard_map/dot_general | solution.py:113
  1383.6 17.1 reshape.180
  1400.6 15.9 fusion.50
  1423.7 15.3 multiply_convert_fusion
  1442.1 44.3 %all-gather = bf16[2048,132]{0,1:T(8,128)(2,1)S(1)} all-gather(bf16[1024,132]{0,1:T(8,128)(2,1)S(1)} %convolution_convert_fusion.4), channel_id=2, replica_groups=mesh['rep'=8,'tr'=8,'tc'=2] {'tc'}, dimensions={0}, use_global_device_ids=true | all-gather | bytes 811008 | tf_op jit(solution)/shard_map/all_gather | solution.py:180
  1488.2 6.7 compare_select_fusion
  1498.2 7.6 copy.163
  1506.3 6.0 broadcast_in_dim.164
  1512.3 155.8 %while.23 = (s32[]{:T(128)}, f32[128,16,1600]{2,1,0:T(8,128)}, f32[8,128,1600]{2,1,0:T(8,128)}, f32[8,128,1600]{2,0,1:T(8,128)}, f32[16,1600]{1,0:T(8,128)S(1)},...) while((s32[]{:T(128)}, f32[128,16,1600]{2,1,0:T(8,128)}, ...), condition=%wide.region_17.18_spmd, body=%wide.region_15.17_spmd.sunk | while | flops 20070400 | bytes 37087612 | solution.py:212
  1517.2 12.4 multiply_reduce_fusion.3
  1536.7 12.4 multiply_reduce_fusion.3
  1556.1 12.4 multiply_reduce_fusion.3
  1575.6 12.4 multiply_reduce_fusion.3
  1595.1 12.4 multiply_reduce_fusion.3
  1614.5 12.4 multiply_reduce_fusion.3
  1634.1 12.4 multiply_reduce_fusion.3
  1653.6 12.4 multiply_reduce_fusion.3
  1673.0 8.1 fusion.34
  1681.2 7.5 convolution_convert_fusion
  1689.2 4.9 copy.172
  1696.1 10.4 reduce-scatter.5.cloned.1.call-done
  (346 shorter events, 214.2 us)
Async XLA Ops:
  6.5 298.2 %all-gather.14.cloned.1.call-start = ((), (), s32[]{:S(2)}) async-start(), calls=%async_computation.9 | async-start | bytes 2129920 | tf_op jit(solution)/shard_map/all_gather | solution.py:107
  7.3 626.2 %all-gather.16.cloned.1.call-start = ((), (), s32[]{:S(2)}) async-start(), calls=%async_computation.10 | async-start | bytes 2129920 | tf_op jit(solution)/shard_map/all_gather | solution.py:225
  8.0 42.6 %copy-start.13 = (f32[800]{0:T(1024)S(1)}, f32[800]{0:T(1024)}, u32[]{:S(2)}) copy-start(f32[800]{0:T(1024)} %param.33) | copy-start | bytes 9604
  8.0 687.5 %all-gather.12.cloned.1.call-start = ((), (), s32[]{:S(2)}) async-start(), calls=%async_computation.6 | async-start | bytes 4915200 | tf_op jit(solution)/shard_map/all_gather | solution.py:103
  46.2 11.8 copy-start.6
  53.5 10.2 copy-start.8
  53.5 11.3 copy-start.11
  57.3 173.1 %copy-start.5 = (f32[8,3,1600]{2,0,1:T(8,128)S(1)}, f32[8,3,1600]{2,0,1:T(8,128)}, u32[]{:S(2)}) copy-start(f32[8,3,1600]{2,0,1:T(8,128)} %param.29) | copy-start | bytes 460804
  57.4 174.6 %copy-start.10 = (f32[4,1600]{1,0:T(4,128)S(1)}, f32[4,1600]{1,0:T(4,128)}, u32[]{:S(2)}) copy-start(f32[4,1600]{1,0:T(4,128)} %param.37) | copy-start | bytes 76804
  57.4 174.7 %copy-start.16 = (s32[512]{0:T(512)S(1)}, s32[512]{0:T(512)}, u32[]{:S(2)}) copy-start(s32[512]{0:T(512)} %param.31) | copy-start | bytes 6148
  57.4 174.7 %copy-start.17 = (s32[512]{0:T(512)S(1)}, s32[512]{0:T(512)}, u32[]{:S(2)}) copy-start(s32[512]{0:T(512)} %param.30) | copy-start | bytes 6148
  57.4 175.4 %copy-start.9 = (f32[16,1600]{1,0:T(8,128)S(1)}, f32[16,1600]{1,0:T(8,128)}, u32[]{:S(2)}) copy-start(f32[16,1600]{1,0:T(8,128)} %param.42) | copy-start | bytes 307204
  57.4 939.5 %all-gather.20.cloned.1.call-start = ((), (), s32[]{:S(2)}) async-start(), calls=%async_computation.12 | async-start | bytes 6922240 | tf_op jit(solution)/shard_map/all_gather | solution.py:226
  59.7 174.0 %all-to-all-start.1 = ((bf16[8,256,256]{2,1,0:T(8,128)(2,1)}), bf16[8,256,256]{2,1,0:T(8,128)(2,1)S(1)}, u32[]{:S(2)}, u32[]{:S(2)}) async-start(bf16[8,256,256]{2,1,0:T(8,128)(2,1)} %broadcast_select_fusion.1), calls=%async_computation.1 | async-start | bytes 2097152 | tf_op jit(solution)/shard_map/all_to_all | solution.py:79
  63.7 1288.6 %all-gather.18.cloned.1.call-start = ((), (), s32[]{:S(2)}) async-start(), calls=%async_computation.11 | async-start | bytes 13312000 | tf_op jit(solution)/shard_map/all_gather | solution.py:109
  233.7 1186.2 %all-to-all-start.3 = ((bf16[8,3,1600]{2,1,0:T(4,128)(2,1)}), bf16[8,3,1600]{2,1,0:T(4,128)(2,1)S(1)}, u32[]{:S(2)}, u32[]{:S(2)}) async-start(bf16[8,3,1600]{2,1,0:T(4,128)(2,1)} %copy.162), calls=%async_computation.4 | async-start | bytes 212992 | tf_op jit(solution)/shard_map/all_to_all | solution.py:91
  237.1 1457.0 %reduce-scatter.3.cloned.1.call-start = ((), (), s32[]{:S(2)}) async-start(), calls=%async_computation.7 | async-start | bytes 4915200 | tf_op jit(solution)/shard_map/reduce_scatter | solution.py:231
  1416.6 7.2 copy-start.12
  1420.0 86.4 %all-to-all-start.2 = ((bf16[8,16,1600]{2,1,0:T(8,128)(2,1)}), bf16[8,16,1600]{2,1,0:T(8,128)(2,1)S(1)}, u32[]{:S(2)}, u32[]{:S(2)}) async-start(bf16[8,16,1600]{2,1,0:T(8,128)(2,1)} %select_convert_fusion), calls=%async_computation.3 | async-start | bytes 851968 | tf_op jit(solution)/shard_map/all_to_all | solution.py:84
  1423.4 283.0 %reduce-scatter.5.cloned.1.call-start = ((), (), s32[]{:S(2)}) async-start(), calls=%async_computation.8 | async-start | bytes 4915200 | tf_op jit(solution)/shard_map/reduce_scatter | solution.py:234
  1423.7 17.1 copy-start.19
  1439.1 49.1 %copy-start.20 = (bf16[100,1600]{1,0:T(8,128)(2,1)S(1)}, bf16[100,1600]{1,0:T(8,128)(2,1)}, u32[]{:S(2)}) copy-start(bf16[100,1600]{1,0:T(8,128)(2,1)} %param.40) | copy-start | bytes 960004
  1439.1 49.1 %copy-start.21 = (f32[1600]{0:T(1024)S(1)}, f32[1600]{0:T(1024)}, u32[]{:S(2)}) copy-start(f32[1600]{0:T(1024)} %param.41) | copy-start | bytes 19204
  1488.2 6.7 copy-start.3
  1506.3 6.0 copy-start.7
  1668.1 4.9 copy-start.4
  1668.1 13.0 slice-start
  1673.0 8.2 slice-start.1
  1681.2 7.6 copy-start.14
  1681.2 7.7 copy-start.15
  1681.2 7.7 copy-start.18
  1694.1 23.2 %copy-start.1 = (bf16[8,16,8,800]{3,2,1,0:T(8,128)(2,1)S(1)}, bf16[8,16,8,800]{3,2,1,0:T(8,128)(2,1)}, u32[]{:S(2)}) copy-start(bf16[8,16,8,800]{3,2,1,0:T(8,128)(2,1)} %param.26) | copy-start | bytes 4915204
  (2 other events, 5.0 us)
Sparse Core Ops, SparseCore 0:
  9.0 295.6 all-gather.13
  306.4 327.0 all-gather.15
  635.1 60.3 all-gather.11
  697.0 299.8 all-gather.19
  998.4 353.9 all-gather.17
  1354.6 55.2 reduce-scatter.2
  1688.9 17.5 reduce-scatter.4
